TPU v7x, 32 devices: a whole 2x2x4 slice. The times are simulated.
32 devices in a mesh: frames: 8 (over y, x, core), chan: 4 (over z).
Axes of the slice: x: 2, y: 2, z: 4, core: 2. Of those that a mesh axis runs over, the one named last changes fastest.
Arguments:
- inputs: bfloat16 [16, 256, 16, 128], P('frames', 'chan'), may hold values from -6 to 6
- saved: bfloat16 [16, 256, 16, 128], P('frames', 'chan'), may hold values from -6 to 6
- cotangent: bfloat16 [8, 256, 512], P('frames', 'chan'), may hold values from -24 to 24
- spatial_w: bfloat16 [3, 3, 256, 256], P(None, None, 'chan'), may hold values from -0.125 to 0.125
- temporal_w: bfloat16 [3, 256, 256], replicated, may hold values from -0.21875 to 0.21875
Outputs:
- input_grad: bfloat16 [16, 256, 16, 128], P('frames', 'chan')
- spatial_grad: float32 [3, 3, 256, 256], P(None, None, 'chan')
- temporal_grad: float32 [3, 256, 256], P(None, 'chan')
All inputs are finite; a program needn't handle non-finite values.
Results may differ from a plain program's by a relative error of at most 0.0049.
Values may be sent and summed in bfloat16 or wider, within the bound.
No kernel may reach another device: no remote copies, remote signals or barrier semaphores. Data moves between devices by JAX's collectives and lax.ppermute only.
A program may use at most 64 MiB of HBM per device.

v0:
```python
import math
import jax
import jax.numpy as jnp
from jax import lax
from jax.sharding import PartitionSpec as P


def temporal_terms(saved_ext, grad_ext, temporal_w, row_total, frame_count):
    result = jnp.zeros((frame_count, row_total, grad_ext.shape[2]), jnp.float32)
    for tap in range(3):
        result = result + jnp.einsum(
            "fol,io->fil",
            grad_ext[2 - tap : 2 - tap + frame_count],
            temporal_w[tap],
            preferred_element_type=jnp.float32,
        )
    partial_value = jnp.stack(
        [
            jnp.einsum(
                "fil,fol->io",
                saved_ext[tap : tap + frame_count],
                grad_ext[1 : frame_count + 1],
                preferred_element_type=jnp.float32,
            )
            for tap in range(3)
        ]
    )
    return (result.astype(jnp.bfloat16), partial_value)


def shards(inputs, saved, cotangent, spatial_w, temporal_w):
    frame_count, quarter, row_count, col_count = inputs.shape
    channels = temporal_w.shape[1]
    row_half, col_half = (row_count // 2, col_count // 2)
    scale = 1.0 / math.sqrt(frame_count * lax.axis_size("frames") * row_count * col_count)
    full_cot = lax.all_gather(cotangent, "chan", axis=1, tiled=True)
    row_first, row_total = (0, channels)
    frame_pad = ((1, 1), (0, 0), (0, 0))
    pooled_saved = saved.reshape(frame_count, quarter, row_half, 2, col_half, 2).transpose(
        0, 1, 3, 5, 2, 4
    )
    pooled_saved = pooled_saved.reshape(frame_count, quarter, 4, row_half * col_half)
    pooled_cot = full_cot.reshape(1, channels, 1, row_half * col_half)
    moved_saved, moved_cot = (
        lax.all_to_all(pooled_saved, "frames", split_axis=3, concat_axis=0, tiled=True),
        lax.all_to_all(pooled_cot, "frames", split_axis=3, concat_axis=0, tiled=True),
    )
    frame_total, local_cells = (moved_saved.shape[0], moved_saved.shape[3])
    spread = jnp.broadcast_to(moved_cot[:, None], (frame_total // 2, 2, channels, 4, local_cells))
    upsampled = (
        spread.reshape(frame_total, channels, 4 * local_cells).astype(jnp.float32) * 0.125
    ).astype(jnp.bfloat16)
    grad_ext = jnp.pad(upsampled, frame_pad)
    saved_ext = jnp.pad(moved_saved.reshape(frame_total, quarter, 4 * local_cells), frame_pad)
    cell_grad, temporal_part = temporal_terms(
        saved_ext, grad_ext, temporal_w, row_total, frame_total
    )
    cell_grad = cell_grad.reshape(frame_total, row_total, 4, local_cells)
    back_grad = lax.all_to_all(cell_grad, "frames", split_axis=0, concat_axis=3, tiled=True)
    back_grad = back_grad.reshape(frame_count, row_total, 2, 2, row_half, col_half).transpose(
        0, 1, 4, 2, 5, 3
    )
    saved_grad = back_grad.reshape(frame_count, row_total, row_count, col_count)
    temporal_total = lax.psum(temporal_part, "frames")
    space_pad = ((0, 0), (0, 0), (1, 1), (1, 1))
    grad_pad = jnp.pad(saved_grad, space_pad)
    input_pad = jnp.pad(inputs, space_pad)
    input_sum = jnp.zeros((frame_count, quarter, row_count, col_count), jnp.float32)
    kernel_rows = []
    for tap_row in range(3):
        kernel_cols = []
        for tap_col in range(3):
            window = grad_pad[
                :, :, 2 - tap_row : 2 - tap_row + row_count, 2 - tap_col : 2 - tap_col + col_count
            ]
            input_sum = input_sum + jnp.einsum(
                "fohw,io->fihw",
                window,
                spatial_w[tap_row, tap_col],
                preferred_element_type=jnp.float32,
            )
            shifted = input_pad[:, :, tap_row : tap_row + row_count, tap_col : tap_col + col_count]
            kernel_cols.append(
                jnp.einsum("fihw,fohw->io", shifted, saved_grad, preferred_element_type=jnp.float32)
            )
        kernel_rows.append(jnp.stack(kernel_cols))
    spatial_part = jnp.stack(kernel_rows)
    spatial_total = lax.psum(spatial_part, "frames")
    return (input_sum.astype(jnp.bfloat16), spatial_total * scale, temporal_total * scale)


def solution(mesh):
    return jax.shard_map(
        shards,
        mesh=mesh,
        in_specs=(
            P("frames", "chan", None, None),
            P("frames", "chan", None, None),
            P("frames", "chan", None),
            P(None, None, "chan", None),
            P(),
        ),
        out_specs=(
            P("frames", "chan", None, None),
            P(None, None, "chan", None),
            P(None, "chan", None),
        ),
        check_vma=False,
    )
```

profile of v0, /device:TPU:0, one launch (start us, length us, event | category | flops | bytes accessed | tf_op | source)
XLA Modules:
  0.0 170.7 jit_solution(4398962847321769897)
XLA Ops:
  7.2 16.0 %all_gather.3 = bf16[1,256,512]{2,1,0:T(8,128)(2,1)S(1)} all-gather(bf16[1,64,512]{2,1,0:T(8,128)(2,1)} %param.7), channel_id=1, replica_groups=mesh['frames'=8,'chan'=4] {'chan'}, dimensions={1}, use_global_device_ids=true | all-gather | bytes 327680 | tf_op jit(solution)/shard_map/all_gather | solution.py:36
  23.6 0.5 broadcast.35
  24.1 2.2 %reduce = bf16[512,256]{1,0:T(8,128)(2,1)S(1)} reduce(bf16[512,1,1,256]{3,2,1,0:T(2,128)(2,1)S(1)} %bitcast.212, bf16[]{:T(256)} %broadcast.35), dimensions={1,2}, to_apply=%bitcast.179.reduce_sub_computation | reduce | bytes 524290
  26.3 0.8 reshape.84
  27.1 3.7 %all-to-all-start = ((bf16[8,2,8192]{2,1,0:T(2,128)(2,1)}), bf16[8,2,8192]{2,1,0:T(2,128)(2,1)S(1)}, u32[]{:S(2)}, u32[]{:S(2)}) async-start(bf16[8,2,8192]{2,1,0:T(2,128)(2,1)} %reshape.84), calls=%async_computation | async-start | bytes 524288 | tf_op jit(solution)/shard_map/all_to_all | solution.py:46
  30.8 0.6 copy.77
  31.4 0.7 copy.108
  32.1 1.5 reshape.86
  33.6 4.1 %all-to-all-done = bf16[8,2,8192]{2,1,0:T(2,128)(2,1)S(1)} async-done(((bf16[8,2,8192]{2,1,0:T(2,128)(2,1)}), bf16[8,2,8192]{2,1,0:T(2,128)(2,1)S(1)}, u32[]{:S(2)}, u32[]{:S(2)}) %all-to-all-start) | async-done | bytes 262176 | tf_op jit(solution)/shard_map/all_to_all | solution.py:46
  37.7 3.5 %all-to-all-start.2 = ((bf16[8,2,16384]{2,1,0:T(2,128)(2,1)}), bf16[8,2,16384]{2,1,0:T(2,128)(2,1)S(1)}, u32[]{:S(2)}, u32[]{:S(2)}) async-start(bf16[8,2,16384]{2,1,0:T(2,128)(2,1)} %reshape.86), calls=%async_computation.2 | async-start | bytes 1048576 | tf_op jit(solution)/shard_map/all_to_all | solution.py:45
  41.8 0.7 copy-done.2
  42.5 0.7 fusion.20
  43.3 0.7 fusion.22
  44.0 2.1 %add_convert_fusion = bf16[16,256,256]{2,1,0:T(8,128)(2,1)} fusion(f32[16,256,256]{2,1,0:T(8,128)S(1)} %fusion.22, f32[16,256,256]{2,1,0:T(8,128)S(1)} %fusion.20, bf16[16,256,256]{1,2,0:T(8,128)(2,1)S(1)} %bitcast.202, bf16[3,256,256]{2,1,0:T(8,128)(2,1)S(1)} %copy-done.2), kind=kOutput, calls=%fused_computation.8 | convolution fusion | flops 506462208 | bytes 12713984 | tf_op jit(solution)/shard_map/fol,io->fil/dot_general | solution.py:11
  46.1 4.8 %all-to-all-done.2 = bf16[8,2,16384]{2,1,0:T(2,128)(2,1)S(1)} async-done(((bf16[8,2,16384]{2,1,0:T(2,128)(2,1)}), bf16[8,2,16384]{2,1,0:T(2,128)(2,1)S(1)}, u32[]{:S(2)}, u32[]{:S(2)}) %all-to-all-start.2) | async-done | bytes 524320 | tf_op jit(solution)/shard_map/all_to_all | solution.py:45
  50.9 4.4 %all-to-all-start.1 = ((bf16[16,256,4,64]{1,3,2,0:T(8,128)(2,1)}), bf16[16,256,4,64]{1,3,2,0:T(8,128)(2,1)}, u32[]{:S(2)}, u32[]{:S(2)}) async-start(bf16[16,256,4,64]{1,3,2,0:T(8,128)(2,1)} %bitcast.205), calls=%async_computation.1 | async-start | bytes 4194304 | tf_op jit(solution)/shard_map/all_to_all | solution.py:59
  55.5 1.2 copy.66
  56.7 1.7 reshape.87
  58.3 2.4 %copy.81 = bf16[2,64,4,8,64]{4,1,2,0,3:T(8,128)(2,1)} copy(bf16[2,64,4,8,64]{1,2,0,4,3:T(4,128)(2,1)} %bitcast.209) | data formatting | bytes 1048576 | tf_op jit(solution)/shard_map/all_to_all | solution.py:45
  60.7 3.1 %copy.82 = bf16[8,2,64,4,64]{4,3,2,1,0:T(4,128)(2,1)} copy(bf16[8,2,64,4,64]{4,2,3,1,0:T(8,128)(2,1)} %bitcast.207) | data formatting | bytes 1048576 | tf_op jit(solution)/shard_map/all_to_all | solution.py:45
  63.9 2.1 %reshape.55 = bf16[16,64,256]{2,1,0:T(8,128)(2,1)S(1)} reshape(bf16[8,2,64,4,64]{4,3,2,1,0:T(4,128)(2,1)} %copy.82) | data formatting | bytes 1048576 | tf_op jit(solution)/shard_map/reshape | solution.py:54
  65.9 1.7 %convolution_bitcast_fusion = f32[1,64,256]{2,1,0:T(8,128)S(1)} fusion(bf16[8,256,64]{1,2,0:T(8,128)(2,1)S(1)} %bitcast.214, bf16[2,64,4,8,64]{4,1,2,0,3:T(8,128)(2,1)} %copy.81), kind=kOutput, calls=%fused_computation.35 | convolution fusion | flops 134217728 | bytes 851968 | tf_op jit(solution)/shard_map/fil,fol->io/dot_general | solution.py:19
  68.7 0.7 pad_maximum_fusion.1
  69.4 12.5 %all-to-all-done.1 = bf16[16,256,4,64]{1,3,2,0:T(8,128)(2,1)} async-done(((bf16[16,256,4,64]{1,3,2,0:T(8,128)(2,1)}), bf16[16,256,4,64]{1,3,2,0:T(8,128)(2,1)}, u32[]{:S(2)}, u32[]{:S(2)}) %all-to-all-start.1) | async-done | bytes 2097184 | tf_op jit(solution)/shard_map/all_to_all | solution.py:59
  81.9 5.1 %copy.63 = bf16[2,256,8,2,64,2]{1,0,5,4,3,2:T(2,128)(2,1)} copy(bf16[2,256,8,2,64,2]{1,4,5,3,0,2:T(8,128)(2,1)} %bitcast.17) | data formatting | bytes 4194304 | tf_op jit(solution)/shard_map/transpose | solution.py:60
  87.0 5.1 %copy.64 = bf16[2,256,16,128]{3,1,2,0:T(8,128)(2,1)S(1)} copy(bf16[2,256,16,128]{1,0,3,2:T(2,128)(2,1)} %bitcast.206) | data formatting | bytes 4194304 | tf_op jit(solution)/shard_map/reshape | solution.py:63
  92.0 0.8 convolution_bitcast_fusion.10
  92.8 0.8 convolution_bitcast_fusion.11
  93.6 0.8 convolution_bitcast_fusion.6
  94.3 0.8 convolution_bitcast_fusion.8
  95.1 0.8 convolution_bitcast_fusion.9
  95.9 0.8 convolution_bitcast_fusion.7
  96.6 0.8 convolution_bitcast_fusion.3
  97.4 0.8 convolution_bitcast_fusion.4
  98.2 0.8 convolution_bitcast_fusion.5
  98.9 0.7 fusion
  99.7 0.5 fusion.31
  100.6 0.8 fusion.14
  101.4 0.9 fusion.13
  102.2 0.8 fusion.11
  103.0 0.8 fusion.10
  103.9 0.9 pad_maximum_fusion
  104.8 0.5 fusion.9
  105.3 0.8 fusion.17
  106.1 1.1 copy.85
  107.2 53.1 %all-reduce.7.cloned.1.call-done = (f32[3,3,64,256]{3,2,1,0:T(8,128)}, f32[3,64,256]{2,1,0:T(8,128)}) async-done(((f32[3,3,64,256]{3,2,1,0:T(8,128)}, f32[3,64,256]{2,1,0:T(8,128)}), (f32[3,3,64,256]{3,2,1,0:T(8,128)}, f32[3,64,256]{2,1,0:T(8,128)})) %all-reduce.7.cloned.1.call-update) | async-done | bytes 786448 | tf_op jit(solution)/shard_map/psum | solution.py:88
  160.3 1.9 %broadcast_multiply_fusion = f32[3,3,64,256]{3,2,1,0:T(8,128)} fusion(f32[3,3,64,256]{3,2,1,0:T(8,128)} %get-tuple-element.15), kind=kLoop, calls=%fused_computation.50 | loop fusion | flops 147456 | bytes 1179648 | tf_op jit(solution)/shard_map/mul | solution.py:89
  162.3 1.6 broadcast_multiply_fusion.1
  (18 shorter events, 2.7 us)
Async XLA Ops:
  7.2 23.7 %copy-start.1 = (bf16[2,64,16,128]{3,2,1,0:T(8,128)(2,1)S(1)}, bf16[2,64,16,128]{3,2,1,0:T(8,128)(2,1)}, u32[]{:S(2)}) copy-start(bf16[2,64,16,128]{3,2,1,0:T(8,128)(2,1)} %param.6) | copy-start | bytes 1572868
  27.1 10.6 %all-to-all-start = ((bf16[8,2,8192]{2,1,0:T(2,128)(2,1)}), bf16[8,2,8192]{2,1,0:T(2,128)(2,1)S(1)}, u32[]{:S(2)}, u32[]{:S(2)}) async-start(bf16[8,2,8192]{2,1,0:T(2,128)(2,1)} %reshape.84), calls=%async_computation | async-start | bytes 524288 | tf_op jit(solution)/shard_map/all_to_all | solution.py:46
  37.7 13.2 %all-to-all-start.2 = ((bf16[8,2,16384]{2,1,0:T(2,128)(2,1)}), bf16[8,2,16384]{2,1,0:T(2,128)(2,1)S(1)}, u32[]{:S(2)}, u32[]{:S(2)}) async-start(bf16[8,2,16384]{2,1,0:T(2,128)(2,1)} %reshape.86), calls=%async_computation.2 | async-start | bytes 1048576 | tf_op jit(solution)/shard_map/all_to_all | solution.py:45
  41.5 1.0 copy-start.2
  50.9 31.0 %all-to-all-start.1 = ((bf16[16,256,4,64]{1,3,2,0:T(8,128)(2,1)}), bf16[16,256,4,64]{1,3,2,0:T(8,128)(2,1)}, u32[]{:S(2)}, u32[]{:S(2)}) async-start(bf16[16,256,4,64]{1,3,2,0:T(8,128)(2,1)} %bitcast.205), calls=%async_computation.1 | async-start | bytes 4194304 | tf_op jit(solution)/shard_map/all_to_all | solution.py:59
  55.2 105.1 %all-reduce.7.cloned.1.call-start = ((), (), s32[]{:S(2)}) async-start(), calls=%async_computation.3 | async-start | bytes 1572864 | tf_op jit(solution)/shard_map/psum | solution.py:88
  94.3 1.5 copy-start
  97.4 1.5 copy-start.3
Sparse Core Ops, SparseCore 0:
  104.9 55.3 all-reduce.6
where the time goes:
time: 172 us; the launch traced here: 171 us
  waiting for transfers between devices  74.6 us (43%)
  local copies, waits for them, and re-layouts  27.5 us (16%)
  matrix products  19.2 us (11%)
  blocking collectives  16 us (9%)
  between operations  14.3 us (8%)
  starting transfers between devices  11.8 us (7%)
  other arithmetic  7.4 us (4%)
    psum x1, waiting for transfers between devices, shards(): spatial_total = lax.psum(spatial_part, 'frames')  53.1 us
    all_gather x1, blocking collectives, shards(): full_cot = lax.all_gather(cotangent, 'chan', axis=1, tiled=True)  16 us
    all_to_all x1, waiting for transfers between devices, shards(): lax.all_to_all(cell_grad, 'frames', split_axis=0, concat_axis=3, tiled=True)  12.5 us
    unnamed x16, local copies, waits for them, and re-layouts  8.32 us
    dot_general x9, matrix products, shards(): jnp.einsum('fihw,fohw->io', shifted, saved_grad, preferred_element_type=j...  6.84 us
    dot_general x9, matrix products, shards(): jnp.einsum('fohw,io->fihw', window, spatial_w[tap_row, tap_col], preferre...  6.16 us
    all_to_all x2, local copies, waits for them, and re-layouts, shards(): lax.all_to_all(pooled_saved, 'frames', split_axis=3, concat_axis=0, tiled...  5.53 us
    transpose x1, local copies, waits for them, and re-layouts, shards(): back_grad.reshape(frame_count, row_total, 2, 2, row_half, col_half)  5.08 us
  transfers between devices with their start and end apart: 4, of which 4 were waited for; matrix products, arithmetic and copies ran while one was open for 14% of the time, Pallas kernels for 0%

commit v1 on v0

--- a/solution.py
+++ b/solution.py
@@ -85,7 +85,13 @@
             )
         kernel_rows.append(jnp.stack(kernel_cols))
     spatial_part = jnp.stack(kernel_rows)
-    spatial_total = lax.psum(spatial_part, "frames")
+    size = lax.axis_size("frames")
+    spatial_total, reach = (spatial_part, 1)
+    while reach < size:
+        spatial_total = spatial_total + lax.ppermute(
+            spatial_total, "frames", [(i, i ^ reach) for i in range(size)]
+        )
+        reach = 2 * reach
     return (input_sum.astype(jnp.bfloat16), spatial_total * scale, temporal_total * scale)
 
 

time: 172 us -> 183 us (1.064)
  waiting for transfers between devices: 74.6 us -> 88.3 us
  local copies, waits for them, and re-layouts: 27.5 us -> 25.4 us
  starting transfers between devices: 11.8 us -> 13.7 us
    ppermute x0 -> x3, waiting for transfers between devices: none -> 22.9 us  [shards(): lax.ppermute(spatial_total, 'frames', [(i, i ^ reach) for i in range(size)])]
    all_to_all x1, waiting for transfers between devices: 12.5 us -> 0.01 us  [shards(): lax.all_to_all(cell_grad, 'frames', split_axis=0, concat_axis=3, tiled=True)]
    psum x1, waiting for transfers between devices: 53.1 us -> 56.4 us  [shards(): temporal_total = lax.psum(temporal_part, 'frames')]
    all_to_all x2, local copies, waits for them, and re-layouts: 5.53 us -> 3.59 us  [shards(): lax.all_to_all(pooled_saved, 'frames', split_axis=3, concat_axis=0, tiled...]
    ppermute x0 -> x3, starting transfers between devices: none -> 1.9 us  [shards(): lax.ppermute(spatial_total, 'frames', [(i, i ^ reach) for i in range(size)])]
    unnamed x16 -> x18, local copies, waits for them, and re-layouts: 8.32 us -> 8.2 us
  transfers between devices with their start and end apart: 4 -> 7, of which waited for: 4 -> 6; matrix products, arithmetic and copies ran while one was open for 14% -> 15% of each run, Pallas kernels for 0% -> 0%
where the time goes in v1:
time: 183 us
  waiting for transfers between devices  88.3 us (48%)
  local copies, waits for them, and re-layouts  25.4 us (14%)
  matrix products  19.2 us (10%)
  blocking collectives  16 us (9%)
  between operations  14.3 us (8%)
  starting transfers between devices  13.7 us (7%)
  other arithmetic  5.75 us (3%)
    psum x1, waiting for transfers between devices, shards(): temporal_total = lax.psum(temporal_part, 'frames')  56.4 us
    ppermute x3, waiting for transfers between devices, shards(): lax.ppermute(spatial_total, 'frames', [(i, i ^ reach) for i in range(size)])  22.9 us
    all_gather x1, blocking collectives, shards(): full_cot = lax.all_gather(cotangent, 'chan', axis=1, tiled=True)  16 us
    unnamed x18, local copies, waits for them, and re-layouts  8.2 us
    dot_general x9, matrix products, shards(): jnp.einsum('fihw,fohw->io', shifted, saved_grad, preferred_element_type=j...  6.84 us
    dot_general x9, matrix products, shards(): jnp.einsum('fohw,io->fihw', window, spatial_w[tap_row, tap_col], preferre...  6.17 us
    reshape x1, local copies, waits for them, and re-layouts, shards(): saved_grad = back_grad.reshape(frame_count, row_total, row_count, col_count)  5.07 us
    transpose x1, local copies, waits for them, and re-layouts, shards(): back_grad.reshape(frame_count, row_total, 2, 2, row_half, col_half)  5.07 us
  transfers between devices with their start and end apart: 7, of which 6 were waited for; matrix products, arithmetic and copies ran while one was open for 15% of the time, Pallas kernels for 0%

profile of v1, /device:TPU:0, one launch (start us, length us, event | category | flops | bytes accessed | tf_op | source)
XLA Modules:
  0.0 182.7 jit_solution(14169580845108747358)
XLA Ops:
  7.2 16.0 %all_gather.3 = bf16[1,256,512]{2,1,0:T(8,128)(2,1)S(1)} all-gather(bf16[1,64,512]{2,1,0:T(8,128)(2,1)} %param.7), channel_id=1, replica_groups=mesh['frames'=8,'chan'=4] {'chan'}, dimensions={1}, use_global_device_ids=true | all-gather | bytes 327680 | tf_op jit(solution)/shard_map/all_gather | solution.py:36
  23.6 0.5 broadcast.35
  24.1 2.2 %reduce = bf16[512,256]{1,0:T(8,128)(2,1)S(1)} reduce(bf16[512,1,1,256]{3,2,1,0:T(2,128)(2,1)S(1)} %bitcast.212, bf16[]{:T(256)} %broadcast.35), dimensions={1,2}, to_apply=%bitcast.179.reduce_sub_computation | reduce | bytes 524290
  26.3 0.8 reshape.84
  27.1 3.7 %all-to-all-start = ((bf16[8,2,8192]{2,1,0:T(2,128)(2,1)}), bf16[8,2,8192]{2,1,0:T(2,128)(2,1)S(1)}, u32[]{:S(2)}, u32[]{:S(2)}) async-start(bf16[8,2,8192]{2,1,0:T(2,128)(2,1)} %reshape.84), calls=%async_computation | async-start | bytes 524288 | tf_op jit(solution)/shard_map/all_to_all | solution.py:46
  30.8 0.6 copy.77
  31.4 0.7 copy.108
  32.1 1.5 reshape.86
  33.6 4.1 %all-to-all-done = bf16[8,2,8192]{2,1,0:T(2,128)(2,1)S(1)} async-done(((bf16[8,2,8192]{2,1,0:T(2,128)(2,1)}), bf16[8,2,8192]{2,1,0:T(2,128)(2,1)S(1)}, u32[]{:S(2)}, u32[]{:S(2)}) %all-to-all-start) | async-done | bytes 262176 | tf_op jit(solution)/shard_map/all_to_all | solution.py:46
  37.7 3.5 %all-to-all-start.2 = ((bf16[8,2,16384]{2,1,0:T(2,128)(2,1)}), bf16[8,2,16384]{2,1,0:T(2,128)(2,1)S(1)}, u32[]{:S(2)}, u32[]{:S(2)}) async-start(bf16[8,2,16384]{2,1,0:T(2,128)(2,1)} %reshape.86), calls=%async_computation.2 | async-start | bytes 1048576 | tf_op jit(solution)/shard_map/all_to_all | solution.py:45
  41.8 0.7 copy-done.3
  42.5 0.7 fusion.20
  43.3 0.7 fusion.22
  44.0 2.1 %add_convert_fusion = bf16[16,256,256]{2,1,0:T(8,128)(2,1)} fusion(f32[16,256,256]{2,1,0:T(8,128)S(1)} %fusion.22, f32[16,256,256]{2,1,0:T(8,128)S(1)} %fusion.20, bf16[16,256,256]{1,2,0:T(8,128)(2,1)S(1)} %bitcast.202, bf16[3,256,256]{2,1,0:T(8,128)(2,1)S(1)} %copy-done.3), kind=kOutput, calls=%fused_computation.8 | convolution fusion | flops 506462208 | bytes 12713984 | tf_op jit(solution)/shard_map/fol,io->fil/dot_general | solution.py:11
  46.1 4.8 %all-to-all-done.2 = bf16[8,2,16384]{2,1,0:T(2,128)(2,1)S(1)} async-done(((bf16[8,2,16384]{2,1,0:T(2,128)(2,1)}), bf16[8,2,16384]{2,1,0:T(2,128)(2,1)S(1)}, u32[]{:S(2)}, u32[]{:S(2)}) %all-to-all-start.2) | async-done | bytes 524320 | tf_op jit(solution)/shard_map/all_to_all | solution.py:45
  50.9 4.4 %all-to-all-start.1 = ((bf16[16,256,4,64]{1,3,2,0:T(8,128)(2,1)}), bf16[16,256,4,64]{1,3,2,0:T(8,128)(2,1)}, u32[]{:S(2)}, u32[]{:S(2)}) async-start(bf16[16,256,4,64]{1,3,2,0:T(8,128)(2,1)} %bitcast.205), calls=%async_computation.1 | async-start | bytes 4194304 | tf_op jit(solution)/shard_map/all_to_all | solution.py:59
  55.5 1.6 reshape.87
  57.1 1.7 copy.81
  58.9 1.0 copy-done
  59.8 1.9 %copy.82 = bf16[8,2,64,4,64]{4,3,2,1,0:T(4,128)(2,1)} copy(bf16[8,2,64,4,64]{4,2,3,1,0:T(8,128)(2,1)S(1)} %bitcast.207) | data formatting | bytes 1048576 | tf_op jit(solution)/shard_map/all_to_all | solution.py:45
  61.7 2.1 %reshape.55 = bf16[16,64,256]{2,1,0:T(8,128)(2,1)S(1)} reshape(bf16[8,2,64,4,64]{4,3,2,1,0:T(4,128)(2,1)} %copy.82) | data formatting | bytes 1048576 | tf_op jit(solution)/shard_map/reshape | solution.py:54
  63.8 1.7 convolution_bitcast_fusion
  66.5 0.7 pad_maximum_fusion.1
  67.4 56.4 %all-reduce.6.cloned.1.call-done = f32[3,64,256]{2,1,0:T(8,128)} async-done(((f32[3,64,256]{2,1,0:T(8,128)}), f32[3,64,256]{2,1,0:T(8,128)}) %all-reduce.6.cloned.1.call-update) | async-done | bytes 196624 | tf_op jit(solution)/shard_map/psum | solution.py:64
  123.8 1.6 broadcast_multiply_fusion
  125.4 5.1 %copy.63 = bf16[2,256,8,2,64,2]{1,0,5,4,3,2:T(2,128)(2,1)} copy(bf16[2,256,8,2,64,2]{1,4,5,3,0,2:T(8,128)(2,1)} %bitcast.17) | data formatting | bytes 4194304 | tf_op jit(solution)/shard_map/transpose | solution.py:60
  130.5 5.1 %copy.64 = bf16[2,256,16,128]{3,1,2,0:T(8,128)(2,1)S(1)} copy(bf16[2,256,16,128]{1,0,3,2:T(2,128)(2,1)} %bitcast.206) | data formatting | bytes 4194304 | tf_op jit(solution)/shard_map/reshape | solution.py:63
  135.5 0.8 convolution_bitcast_fusion.10
  136.3 0.8 convolution_bitcast_fusion.11
  137.1 0.8 convolution_bitcast_fusion.6
  137.8 0.8 convolution_bitcast_fusion.8
  138.6 0.8 convolution_bitcast_fusion.9
  139.4 0.8 convolution_bitcast_fusion.7
  140.1 0.8 convolution_bitcast_fusion.3
  140.9 0.8 convolution_bitcast_fusion.4
  141.7 0.8 convolution_bitcast_fusion.5
  142.6 0.7 fusion
  144.7 0.9 collective-permute-start.1
  145.6 0.8 fusion.14
  146.4 0.9 fusion.13
  147.2 0.8 fusion.11
  148.0 12.1 %collective-permute-done.1 = f32[3,3,64,256]{3,2,1,0:T(8,128)S(1)} collective-permute-done((f32[3,3,64,256]{3,2,1,0:T(8,128)S(1)}, f32[3,3,64,256]{3,2,1,0:T(8,128)S(1)}, u32[]{:S(2)}, u32[]{:S(2)}) %collective-permute-start.1) | collective-permute-done | bytes 589856 | tf_op jit(solution)/shard_map/ppermute | solution.py:91
  160.3 0.9 collective-permute-start.2
  161.2 0.8 fusion.10
  162.5 0.8 fusion.17
  163.3 1.1 copy.85
  164.4 10.5 %collective-permute-done.2 = f32[3,3,64,256]{3,2,1,0:T(8,128)S(1)} collective-permute-done((f32[3,3,64,256]{3,2,1,0:T(8,128)S(1)}, f32[3,3,64,256]{3,2,1,0:T(8,128)S(1)}, u32[]{:S(2)}, u32[]{:S(2)}) %collective-permute-start.2) | collective-permute-done | bytes 589856 | tf_op jit(solution)/shard_map/ppermute | solution.py:91
  174.9 0.9 add_multiply_fusion
  (28 shorter events, 4.4 us)
Async XLA Ops:
  7.2 23.7 %copy-start.2 = (bf16[2,64,16,128]{3,2,1,0:T(8,128)(2,1)S(1)}, bf16[2,64,16,128]{3,2,1,0:T(8,128)(2,1)}, u32[]{:S(2)}) copy-start(bf16[2,64,16,128]{3,2,1,0:T(8,128)(2,1)} %param.6) | copy-start | bytes 1572868
  27.1 10.6 %all-to-all-start = ((bf16[8,2,8192]{2,1,0:T(2,128)(2,1)}), bf16[8,2,8192]{2,1,0:T(2,128)(2,1)S(1)}, u32[]{:S(2)}, u32[]{:S(2)}) async-start(bf16[8,2,8192]{2,1,0:T(2,128)(2,1)} %reshape.84), calls=%async_computation | async-start | bytes 524288 | tf_op jit(solution)/shard_map/all_to_all | solution.py:46
  37.7 13.2 %all-to-all-start.2 = ((bf16[8,2,16384]{2,1,0:T(2,128)(2,1)}), bf16[8,2,16384]{2,1,0:T(2,128)(2,1)S(1)}, u32[]{:S(2)}, u32[]{:S(2)}) async-start(bf16[8,2,16384]{2,1,0:T(2,128)(2,1)} %reshape.86), calls=%async_computation.2 | async-start | bytes 1048576 | tf_op jit(solution)/shard_map/all_to_all | solution.py:45
  41.5 1.0 copy-start.3
  50.9 74.5 %all-to-all-start.1 = ((bf16[16,256,4,64]{1,3,2,0:T(8,128)(2,1)}), bf16[16,256,4,64]{1,3,2,0:T(8,128)(2,1)}, u32[]{:S(2)}, u32[]{:S(2)}) async-start(bf16[16,256,4,64]{1,3,2,0:T(8,128)(2,1)} %bitcast.205), calls=%async_computation.1 | async-start | bytes 4194304 | tf_op jit(solution)/shard_map/all_to_all | solution.py:59
  55.2 68.5 %all-reduce.6.cloned.1.call-start = ((), (), s32[]{:S(2)}) async-start(), calls=%async_computation.3 | async-start | bytes 393216 | tf_op jit(solution)/shard_map/psum | solution.py:64
  58.8 1.0 copy-start
  66.0 1.2 copy-start.1
  141.6 1.0 copy-start.4
  142.5 2.1 %collective-permute-start = (f32[3,3,64,256]{3,2,1,0:T(8,128)S(1)}, f32[3,3,64,256]{3,2,1,0:T(8,128)S(1)}, u32[]{:S(2)}, u32[]{:S(2)}) collective-permute-start(f32[3,3,64,256]{3,2,1,0:T(8,128)S(1)} %pad_maximum_fusion), channel_id=1, source_target_pairs={{0,4},{4,0},{8,12},{12,8},{16,20},{20,16},{24,28},{28,24},{1,5},{5... | collective-permute-start | bytes 1769480 | tf_op jit(solution)/shard_map/ppermute | solution.py:91
  144.7 15.5 %collective-permute-start.1 = (f32[3,3,64,256]{3,2,1,0:T(8,128)S(1)}, f32[3,3,64,256]{3,2,1,0:T(8,128)S(1)}, u32[]{:S(2)}, u32[]{:S(2)}) collective-permute-start(f32[3,3,64,256]{3,2,1,0:T(8,128)S(1)} %fusion.64), channel_id=1, source_target_pairs={{0,8},{4,12},{8,0},{12,4},{16,24},{20,28},{24,16},{28,20},{1,9},{5... | collective-permute-start | bytes 1769480 | tf_op jit(solution)/shard_map/ppermute | solution.py:91
  160.3 14.6 %collective-permute-start.2 = (f32[3,3,64,256]{3,2,1,0:T(8,128)S(1)}, f32[3,3,64,256]{3,2,1,0:T(8,128)S(1)}, u32[]{:S(2)}, u32[]{:S(2)}) collective-permute-start(f32[3,3,64,256]{3,2,1,0:T(8,128)S(1)} %fusion.82), channel_id=1, source_target_pairs={{0,16},{4,20},{8,24},{12,28},{16,0},{20,4},{24,8},{28,12},{1,17},{... | collective-permute-start | bytes 1769480 | tf_op jit(solution)/shard_map/ppermute | solution.py:91
Sparse Core Ops, SparseCore 0:
  67.3 56.3 all-reduce.5
